TPU v7x, 32 devices: a whole 2x2x4 slice. The times are simulated.
32 devices in a mesh: groups: 2 (over y), inner: 4 (over z), outer: 4 (over x, core).
Axes of the slice: x: 2, y: 2, z: 4, core: 2. Of those that a mesh axis runs over, the one named last changes fastest.
Arguments:
- queries: bfloat16 [8192, 1024], P(('groups', 'outer', 'inner')), parts along dimension 0, may hold values from -6 to 6
- keys: bfloat16 [8192, 1024], P(('groups', 'outer', 'inner')), parts along dimension 0, may hold values from -6 to 6
- values: bfloat16 [8192, 1024], P(('groups', 'outer', 'inner')), parts along dimension 0, may hold values from -6 to 6
- retain: float32 [8192, 8], P(('groups', 'outer', 'inner')), parts along dimension 0, may hold values from 0.4 to 1
- step: float32 [8192, 8], P(('groups', 'outer', 'inner')), parts along dimension 0, may hold values from 0.000625 to 0.0125
- momentum: float32 [8192, 8], P(('groups', 'outer', 'inner')), parts along dimension 0, may hold values from 0.97 to 0.99
- init_memory: float32 [8, 128, 128], replicated, may hold values from -0.1875 to 0.1875
- init_momentum: float32 [8, 128, 128], replicated, may hold values from -0.1875 to 0.1875
Outputs:
- retrieved: bfloat16 [8192, 1024], P(('groups', 'outer', 'inner')), parts along dimension 0
There are 2 independent parts, one for each index of `groups`. A program takes and returns all parts, laid end to end along the dimension named above; an argument that names none is the same for every part. Nothing has to cross between parts.
All inputs are finite; a program needn't handle non-finite values.
Results may differ from a plain program's by a relative error of at most 0.001.
Values sent between devices are 32-bit elements; how exact they have to be, the bound alone decides.
No kernel may reach another device: no remote copies, remote signals or barrier semaphores. Data moves between devices by JAX's collectives and lax.ppermute only.
A program may use at most 256 MiB of HBM per device.

v0:
```python
import jax
import jax.numpy as jnp
from jax import lax
from jax.sharding import PartitionSpec as P


def carried_in(value, axis, join, neutral):
    count, mine = (lax.axis_size(axis), lax.axis_index(axis))
    pieces = jax.tree.map(lambda part: lax.all_gather(part, axis), value)
    total = jax.tree.map(
        lambda part, zero: jnp.full_like(part, 0) + jnp.asarray(zero, part.dtype), value, neutral
    )

    def turn(position, total):
        longer = join(total, jax.tree.map(lambda part: part[position], pieces))
        return jax.tree.map(lambda new, old: jnp.where(position < mine, new, old), longer, total)

    return lax.fori_loop(0, count - 1, turn, total)


def from_root(block, axis, owner):
    block = jnp.where(lax.axis_index(axis) == owner, block, jnp.zeros_like(block))
    return lax.psum(block, axis)


def unit_rows(source, heads):
    rows = source.astype(jnp.float32).reshape(source.shape[0], heads, -1)
    return rows * lax.rsqrt(jnp.sum(rows * rows, -1, keepdims=True) + 1e-06)


def block_terms(queries, keys, values, retain, step, momentum):
    length = queries.shape[0]
    heads = retain.shape[1]
    precise = lax.Precision.HIGHEST
    query_unit = unit_rows(queries, heads)
    key_unit = unit_rows(keys, heads)
    value_rows = values.astype(jnp.float32).reshape(length, heads, -1)
    key_width = key_unit.shape[2]
    log_retain = jnp.cumsum(jnp.log(retain), 0).T
    log_moment = jnp.cumsum(jnp.log(momentum), 0).T
    position = jnp.arange(length)
    causal = (position[:, None] >= position[None, :])[None]
    retain_decay = jnp.where(
        causal,
        jnp.exp(jnp.where(causal, log_retain[:, :, None] - log_retain[:, None, :], 0.0)),
        0.0,
    )
    momentum_decay = jnp.where(
        causal,
        jnp.exp(jnp.where(causal, log_moment[:, :, None] - log_moment[:, None, :], 0.0)),
        0.0,
    )
    weights = jnp.einsum("htu,hur->htr", retain_decay, momentum_decay, precision=precise)
    carry_scale = jnp.einsum("htu,hu->ht", retain_decay, jnp.exp(log_moment), precision=precise)
    scores = jnp.einsum("thd,rhd->htr", query_unit, key_unit, precision=precise)
    step_rows = step.T
    mixing = scores * weights * step_rows[:, None, :]
    memory_weight = weights[:, -1, :] * step_rows
    moment_weight = jnp.exp(log_moment[:, -1:] - log_moment) * step_rows
    memory_gram = jnp.einsum(
        "rhd,hr,rhe->hde", key_unit, memory_weight, key_unit, precision=precise
    )
    moment_gram = jnp.einsum(
        "rhd,hr,rhe->hde", key_unit, moment_weight, key_unit, precision=precise
    )
    identity = jnp.eye(key_width, dtype=jnp.float32)[None]
    retain_end = jnp.exp(log_retain[:, -1])[:, None, None]
    moment_end = jnp.exp(log_moment[:, -1])[:, None, None]
    carry_end = carry_scale[:, -1][:, None, None]
    upper_rows = jnp.concatenate([retain_end * identity - memory_gram, -moment_gram], axis=2)
    lower_rows = jnp.concatenate([carry_end * identity, moment_end * identity], axis=2)
    transition = jnp.concatenate([upper_rows, lower_rows], axis=1)
    memory_write = jnp.einsum(
        "rhd,hr,rhe->hde", value_rows, memory_weight, key_unit, precision=precise
    )
    moment_write = jnp.einsum(
        "rhd,hr,rhe->hde", value_rows, moment_weight, key_unit, precision=precise
    )
    offset = jnp.concatenate([memory_write, moment_write], axis=2)
    local_terms = (query_unit, key_unit, value_rows, jnp.exp(log_retain), carry_scale, mixing)
    return (transition, offset, local_terms)


def block_output(carried, local_terms):
    query_unit, key_unit, value_rows, retain_scale, carry_scale, mixing = local_terms
    precise = lax.Precision.HIGHEST
    key_width = query_unit.shape[2]
    memory = carried[:, :, :key_width]
    moment_part = carried[:, :, key_width:]
    residual = jnp.einsum("rhd,hed->hre", key_unit, memory, precision=precise) - jnp.transpose(
        value_rows, (1, 0, 2)
    )
    result = retain_scale[:, :, None] * jnp.einsum(
        "thd,hed->hte", query_unit, memory, precision=precise
    )
    result = result + carry_scale[:, :, None] * jnp.einsum(
        "thd,hed->hte", query_unit, moment_part, precision=precise
    )
    result = result - jnp.einsum("htr,hre->hte", mixing, residual, precision=precise)
    return jnp.transpose(result, (1, 0, 2)).reshape(query_unit.shape[0], -1).astype(jnp.bfloat16)


def advance_state(carried, transition, offset):
    return jnp.einsum("hij,hjk->hik", carried, transition, precision=lax.Precision.HIGHEST) + offset


def compose(earlier, later):
    joined = jnp.einsum("hij,hjk->hik", earlier[0], later[0], precision=lax.Precision.HIGHEST)
    return (joined, advance_state(earlier[1], later[0], later[1]))


def apply_earlier(gathered, first_state):
    my_group = lax.axis_index("outer")

    def advance_group(index, carried):
        moved = advance_state(carried, gathered[0][index], gathered[1][index])
        return jnp.where(index < my_group, moved, carried)

    return lax.fori_loop(0, gathered[0].shape[0], advance_group, first_state)


def local(queries, keys, values, retain, step, momentum, init_memory, init_momentum):
    transition, offset, local_terms = block_terms(queries, keys, values, retain, step, momentum)
    identity_maps = (
        jnp.broadcast_to(jnp.eye(transition.shape[1], dtype=jnp.float32), transition.shape),
        jnp.zeros_like(offset),
    )
    before = carried_in((transition, offset), "inner", compose, identity_maps)
    through = compose(before, (transition, offset))
    first_state = jnp.concatenate([init_memory, init_momentum], axis=2)
    last_inner = lax.axis_size("inner") - 1
    group_map = (
        from_root(through[0], "inner", last_inner),
        from_root(through[1], "inner", last_inner),
    )
    gathered = (
        lax.all_gather(group_map[0][None], "outer", axis=0, tiled=True),
        lax.all_gather(group_map[1][None], "outer", axis=0, tiled=True),
    )
    entry_state = apply_earlier(gathered, first_state)
    block_state = advance_state(entry_state, before[0], before[1])
    return block_output(block_state, local_terms)


def solution(mesh):
    placed = (
        P(("groups", "outer", "inner"), None),
        P(("groups", "outer", "inner"), None),
        P(("groups", "outer", "inner"), None),
        P(("groups", "outer", "inner"), None),
        P(("groups", "outer", "inner"), None),
        P(("groups", "outer", "inner"), None),
        P(),
        P(),
    )
    return jax.shard_map(
        local,
        mesh=mesh,
        in_specs=placed,
        out_specs=P(("groups", "outer", "inner"), None),
        check_vma=False,
    )
```

profile of v0, /device:TPU:0, one launch (start us, length us, event | category | flops | bytes accessed | tf_op | source)
XLA Modules:
  0.0 601.0 jit_solution(4477719836671399538)
XLA Ops:
  10.5 2.9 fusion.39
  18.3 2.1 broadcast_multiply_fusion.1
  22.7 2.0 copy.120
  29.2 2.6 copy.125
  32.2 2.3 fusion.44
  38.9 1.8 copy.119
  41.4 74.1 %all-gather.13.cloned.1.call-done = f32[32,128,256]{2,1,0:T(8,128)} async-done(((f32[8,128,256]{2,1,0:T(8,128)}), f32[32,128,256]{2,1,0:T(8,128)}) %all-gather.13.cloned.1.call-update) | async-done | bytes 4194320 | tf_op jit(solution)/shard_map/all_gather | solution.py:9
  115.4 149.8 %all-gather.11.cloned.1.call-done = f32[32,256,256]{2,1,0:T(8,128)} async-done(((f32[8,256,256]{2,1,0:T(8,128)}), f32[32,256,256]{2,1,0:T(8,128)}) %all-gather.11.cloned.1.call-update) | async-done | bytes 8388624 | tf_op jit(solution)/shard_map/all_gather | solution.py:9
  265.4 49.7 %while.30 = (s32[]{:T(128)}, f32[8,256,256]{1,2,0:T(8,128)S(1)}, f32[8,128,256]{1,2,0:T(8,128)}, s32[]{:T(128)}, f32[4,8,256,256]{3,2,1,0:T(8,128)}, /*index=5*/f32[4,8,128,256]{3,2,1,0:T(8,128)}, s32[]{:T(128)}, s32[]{:T(128)}) while((s32[]{:T(128)}, f32[8,256,256]{1,2,0:T(8,128)S(1)}, f32[8,128,256]{1,2,0:T(8,128)}, s32[]{:T(128)}, ...), condition=%wide.region_7.8_spmd.clone, body=%wide.region_6.7_spmd.clone.sunk | while | flops 2417491968 | bytes 25168492 | solution.py:18
  265.4 2.3 constant_dynamic-slice_fusion.5
  270.5 6.1 %fusion.112 = f32[8,128,256]{1,2,0:T(8,128)} fusion(f32[4,8,256,256]{3,2,1,0:T(8,128)} %get-tuple-element.387, s32[]{:T(128)} %get-tuple-element.375, f32[1,8,128,256]{2,3,1,0:T(8,128)S(1)} %copy.193, f32[8,128,256]{1,2,0:T(8,128)S(1)} %copy.218, pred[]{:T(512)S(6)} %compare.3, pred[]{:T(512)S(6)} %lt.44), kind=kOutput, calls=%fused_computation.17.clone.1 | convolution fusion | flops 806354944 | bytes 6293504 | tf_op jit(solution)/shard_map/while/body/eval_jaxpr/hij,hjk->hik/dot_general | solution.py:104
  276.8 5.1 bitcast_select_fusion.2
  281.9 2.3 constant_dynamic-slice_fusion.5
  287.0 6.1 %fusion.112 = f32[8,128,256]{1,2,0:T(8,128)} fusion(f32[4,8,256,256]{3,2,1,0:T(8,128)} %get-tuple-element.387, s32[]{:T(128)} %get-tuple-element.375, f32[1,8,128,256]{2,3,1,0:T(8,128)S(1)} %copy.193, f32[8,128,256]{1,2,0:T(8,128)S(1)} %copy.218, pred[]{:T(512)S(6)} %compare.3, pred[]{:T(512)S(6)} %lt.44), kind=kOutput, calls=%fused_computation.17.clone.1 | convolution fusion | flops 806354944 | bytes 6293504 | tf_op jit(solution)/shard_map/while/body/eval_jaxpr/hij,hjk->hik/dot_general | solution.py:104
  293.3 5.1 bitcast_select_fusion.2
  298.4 2.3 constant_dynamic-slice_fusion.5
  303.5 6.1 %fusion.112 = f32[8,128,256]{1,2,0:T(8,128)} fusion(f32[4,8,256,256]{3,2,1,0:T(8,128)} %get-tuple-element.387, s32[]{:T(128)} %get-tuple-element.375, f32[1,8,128,256]{2,3,1,0:T(8,128)S(1)} %copy.193, f32[8,128,256]{1,2,0:T(8,128)S(1)} %copy.218, pred[]{:T(512)S(6)} %compare.3, pred[]{:T(512)S(6)} %lt.44), kind=kOutput, calls=%fused_computation.17.clone.1 | convolution fusion | flops 806354944 | bytes 6293504 | tf_op jit(solution)/shard_map/while/body/eval_jaxpr/hij,hjk->hik/dot_general | solution.py:104
  309.8 5.1 bitcast_select_fusion.2
  315.1 5.2 fusion.49
  320.3 4.8 select_bitcast_fusion
  325.2 119.8 %all-reduce.3.cloned.1.call-done = (f32[1,8,256,256]{3,2,1,0:T(8,128)}, f32[1,8,128,256]{2,3,1,0:T(8,128)}) async-done(((f32[1,8,256,256]{3,2,1,0:T(8,128)}, f32[1,8,128,256]{2,3,1,0:T(8,128)}), (f32[1,8,256,256]{3,2,1,0:T(8,128)}, f32[1,8,128,256]{2,3,1,0:T(8,128)})) %all-reduce.3.cloned.1.call-update) | async-done | bytes 3145744 | tf_op jit(solution)/shard_map/psum | solution.py:23
  445.0 2.5 copy.133
  452.1 5.1 fusion.66
  458.5 22.6 %all-gather.9.cloned.1.call-done = f32[4,8,128,256]{3,2,1,0:T(8,128)} async-done(((f32[1,8,128,256]{3,2,1,0:T(8,128)}), f32[4,8,128,256]{3,2,1,0:T(8,128)}) %all-gather.9.cloned.1.call-update) | async-done | bytes 4194320 | tf_op jit(solution)/shard_map/all_gather | solution.py:138
  481.2 59.7 %all-gather.7.cloned.1.call-done = f32[4,8,256,256]{3,2,1,0:T(8,128)} async-done(((f32[1,8,256,256]{3,2,1,0:T(8,128)}), f32[4,8,256,256]{3,2,1,0:T(8,128)}) %all-gather.7.cloned.1.call-update) | async-done | bytes 8388624 | tf_op jit(solution)/shard_map/all_gather | solution.py:137
  540.9 41.4 %while.29 = (s32[]{:T(128)}, f32[8,128,256]{1,2,0:T(8,128)}, s32[]{:T(128)}, f32[4,8,256,256]{3,2,1,0:T(8,128)}, f32[4,8,128,256]{3,2,1,0:T(8,128)}, /*index=5*/s32[]{:T(128)}) while((s32[]{:T(128)}, f32[8,128,256]{1,2,0:T(8,128)}, s32[]{:T(128)}, f32[4,8,256,256]{3,2,1,0:T(8,128)}, f32[4,8,128,256]{3,2,1,0:T(8,128)}, ...), condition=%wide.region_11.12_spmd, body=%wide.region_10.11_spmd.sunk | while | flops 805830656 | bytes 16777840 | solution.py:119
  545.3 6.1 %fusion.107 = f32[8,128,256]{1,2,0:T(8,128)} fusion(f32[8,128,256]{1,2,0:T(8,128)S(1)} %copy.216, f32[4,8,256,256]{3,2,1,0:T(8,128)} %get-tuple-element.406, s32[]{:T(128)} %get-tuple-element.397, f32[1,8,128,256]{2,3,1,0:T(8,128)S(1)} %copy-done, pred[]{:T(512)S(6)} %lt.43), kind=kOutput, calls=%fused_computation.5.clone.1 | convolution fusion | flops 805830656 | bytes 6291969 | tf_op jit(solution)/shard_map/while/body/eval_jaxpr/hij,hjk->hik/dot_general | solution.py:104
  555.6 6.1 %fusion.107 = f32[8,128,256]{1,2,0:T(8,128)} fusion(f32[8,128,256]{1,2,0:T(8,128)S(1)} %copy.216, f32[4,8,256,256]{3,2,1,0:T(8,128)} %get-tuple-element.406, s32[]{:T(128)} %get-tuple-element.397, f32[1,8,128,256]{2,3,1,0:T(8,128)S(1)} %copy-done, pred[]{:T(512)S(6)} %lt.43), kind=kOutput, calls=%fused_computation.5.clone.1 | convolution fusion | flops 805830656 | bytes 6291969 | tf_op jit(solution)/shard_map/while/body/eval_jaxpr/hij,hjk->hik/dot_general | solution.py:104
  565.9 6.1 %fusion.107 = f32[8,128,256]{1,2,0:T(8,128)} fusion(f32[8,128,256]{1,2,0:T(8,128)S(1)} %copy.216, f32[4,8,256,256]{3,2,1,0:T(8,128)} %get-tuple-element.406, s32[]{:T(128)} %get-tuple-element.397, f32[1,8,128,256]{2,3,1,0:T(8,128)S(1)} %copy-done, pred[]{:T(512)S(6)} %lt.43), kind=kOutput, calls=%fused_computation.5.clone.1 | convolution fusion | flops 805830656 | bytes 6291969 | tf_op jit(solution)/shard_map/while/body/eval_jaxpr/hij,hjk->hik/dot_general | solution.py:104
  576.2 6.1 %fusion.107 = f32[8,128,256]{1,2,0:T(8,128)} fusion(f32[8,128,256]{1,2,0:T(8,128)S(1)} %copy.216, f32[4,8,256,256]{3,2,1,0:T(8,128)} %get-tuple-element.406, s32[]{:T(128)} %get-tuple-element.397, f32[1,8,128,256]{2,3,1,0:T(8,128)S(1)} %copy-done, pred[]{:T(512)S(6)} %lt.43), kind=kOutput, calls=%fused_computation.5.clone.1 | convolution fusion | flops 805830656 | bytes 6291969 | tf_op jit(solution)/shard_map/while/body/eval_jaxpr/hij,hjk->hik/dot_general | solution.py:104
  582.3 4.0 convolution_add_fusion
  589.4 2.5 fusion.45
  (157 shorter events, 57.5 us)
Async XLA Ops:
  6.5 108.9 %all-gather.13.cloned.1.call-start = ((), (), s32[]{:S(2)}) async-start(), calls=%async_computation.3 | async-start | bytes 5242880 | tf_op jit(solution)/shard_map/all_gather | solution.py:9
  6.6 6.9 %copy-start.25 = (pred[256,256]{1,0:T(8,128)(4,1)}, pred[256,256]{1,0:T(8,128)(4,1)S(1)}, u32[]{:S(2)}) copy-start(pred[256,256]{1,0:T(8,128)(4,1)S(1)} %iota_compare_fusion) | copy-start | bytes 196612
  8.2 5.3 copy-start.28
  10.5 3.0 copy-start.31
  10.5 3.0 copy-start.27
  10.5 4.4 copy-start.21
  18.3 2.1 copy-start.23
  20.4 16.1 %copy-start.2 = (f32[256,8,128]{2,1,0:T(8,128)}, f32[256,8,128]{2,1,0:T(8,128)S(1)}, u32[]{:S(2)}) copy-start(f32[256,8,128]{2,1,0:T(8,128)S(1)} %get-tuple-element.291) | copy-start | bytes 3145732
  24.8 1.7 copy-start.6
  29.2 3.0 copy-start.32
  29.2 3.0 copy-start.26
  29.2 3.0 copy-start.29
  29.2 3.0 copy-start.30
  31.8 233.4 %all-gather.11.cloned.1.call-start = ((), (), s32[]{:S(2)}) async-start(), calls=%async_computation.2 | async-start | bytes 10485760 | tf_op jit(solution)/shard_map/all_gather | solution.py:9
  35.1 2.9 copy-start.8
  35.1 2.9 copy-start.10
  40.7 404.2 %all-reduce.3.cloned.1.call-start = ((), (), s32[]{:S(2)}) async-start(), calls=%async_computation.4 | async-start | bytes 6291456 | tf_op jit(solution)/shard_map/psum | solution.py:23
  315.1 5.2 copy-start.9
  315.1 5.2 copy-start.11
  315.1 5.2 copy-start.13
  315.1 5.2 copy-start.15
  325.2 156.0 %all-gather.9.cloned.1.call-start = ((), (), s32[]{:S(2)}) async-start(), calls=%async_computation.1 | async-start | bytes 5242880 | tf_op jit(solution)/shard_map/all_gather | solution.py:138
  447.5 2.0 copy-start.24
  447.5 93.4 %all-gather.7.cloned.1.call-start = ((), (), s32[]{:S(2)}) async-start(), calls=%async_computation | async-start | bytes 10485760 | tf_op jit(solution)/shard_map/all_gather | solution.py:137
  452.1 5.1 copy-start.1
  543.8 1.5 copy-start
  554.1 1.5 copy-start
  564.4 1.5 copy-start
  574.7 1.5 copy-start
  582.3 4.0 copy-start.4
  586.3 2.5 copy-start.17
  587.6 1.7 copy-start.5
  (9 other events, 9.9 us)
Sparse Core Ops, SparseCore 0:
  31.9 83.4 all-gather.12
  117.0 148.1 all-gather.10
  325.3 119.6 all-reduce.2
  447.7 33.4 all-gather.8
  482.6 58.2 all-gather.6
where the time goes:
time: 609 us; the launch traced here: 601 us
  waiting for transfers between devices  427 us (70%)
  matrix products  93.8 us (15%)
  local copies, waits for them, and re-layouts  56.5 us (9%)
  between operations  13.9 us (2%)
  other arithmetic  8.6 us (1%)
    all_gather x2, waiting for transfers between devices, carried_in(): pieces = jax.tree.map(lambda part: lax.all_gather(part, axis), value)  224 us
    psum x1, waiting for transfers between devices, from_root(): return lax.psum(block, axis)  120 us
    all_gather x1, waiting for transfers between devices, local(): lax.all_gather(group_map[0][None], 'outer', axis=0, tiled=True)  59.7 us
    dot_general x9, matrix products, advance_state(): jnp.einsum('hij,hjk->hik', carried, transition, precision=lax.Precision.H...  51.8 us
    all_gather x1, waiting for transfers between devices, local(): lax.all_gather(group_map[1][None], 'outer', axis=0, tiled=True)  22.6 us
    dot_general x4, matrix products, compose(): jnp.einsum('hij,hjk->hik', earlier[0], later[0], precision=lax.Precision....  20.2 us
  transfers between devices with their start and end apart: 5, of which 5 were waited for; matrix products, arithmetic and copies ran while one was open for 3% of the time, Pallas kernels for 0%

commit v1 on v0

--- a/solution.py
+++ b/solution.py
@@ -2,6 +2,11 @@
 import jax.numpy as jnp
 from jax import lax
 from jax.sharding import PartitionSpec as P
+
+
+def lift_the_panels(panel, bus_axis):
+    z = jnp.sum(lax.all_gather(panel, axis_name=bus_axis), axis=0)
+    return z
 
 
 def carried_in(value, axis, join, neutral):
@@ -20,7 +25,7 @@
 
 def from_root(block, axis, owner):
     block = jnp.where(lax.axis_index(axis) == owner, block, jnp.zeros_like(block))
-    return lax.psum(block, axis)
+    return lift_the_panels(block, axis)
 
 
 def unit_rows(source, heads):

time: 609 us -> 713 us (1.17)
  waiting for transfers between devices: 427 us -> 520 us
  other arithmetic: 8.6 us -> 17.1 us
    all_gather x0 -> x2, waiting for transfers between devices: none -> 219 us  [lift_the_panels(): z = jnp.sum(lax.all_gather(panel, axis_name=bus_axis), axis=0)]
    psum x1 -> x0, waiting for transfers between devices: 120 us -> none  [from_root(): return lax.psum(block, axis)]
    reduce_sum x0 -> x2, other arithmetic: none -> 9.17 us  [lift_the_panels(): z = jnp.sum(lax.all_gather(panel, axis_name=bus_axis), axis=0)]
  transfers between devices with their start and end apart: 5 -> 6, of which waited for: 5 -> 6; matrix products, arithmetic and copies ran while one was open for 3% -> 5% of each run, Pallas kernels for 0% -> 0%
where the time goes in v1:
time: 713 us; the launch traced here: 705 us
  waiting for transfers between devices  520 us (73%)
  matrix products  94.7 us (13%)
  local copies, waits for them, and re-layouts  57.5 us (8%)
  other arithmetic  17.1 us (2%)
  between operations  14.3 us (2%)
    all_gather x2, waiting for transfers between devices, carried_in(): pieces = jax.tree.map(lambda part: lax.all_gather(part, axis), value)  224 us
    all_gather x2, waiting for transfers between devices, lift_the_panels(): z = jnp.sum(lax.all_gather(panel, axis_name=bus_axis), axis=0)  219 us
    all_gather x1, waiting for transfers between devices, local(): lax.all_gather(group_map[0][None], 'outer', axis=0, tiled=True)  59.7 us
    dot_general x9, matrix products, advance_state(): jnp.einsum('hij,hjk->hik', carried, transition, precision=lax.Precision.H...  51.6 us
    dot_general x4, matrix products, compose(): jnp.einsum('hij,hjk->hik', earlier[0], later[0], precision=lax.Precision....  21.4 us
    all_gather x1, waiting for transfers between devices, local(): lax.all_gather(group_map[1][None], 'outer', axis=0, tiled=True)  17.6 us
  transfers between devices with their start and end apart: 6, of which 6 were waited for; matrix products, arithmetic and copies ran while one was open for 5% of the time, Pallas kernels for 0%

profile of v1, /device:TPU:0, one launch (start us, length us, event | category | flops | bytes accessed | tf_op | source)
XLA Modules:
  0.0 705.1 jit_solution(14355368479321419354)
XLA Ops:
  10.5 2.9 fusion.39
  28.6 2.6 copy.121
  31.6 2.3 fusion.44
  40.8 74.1 %all-gather.15.cloned.1.call-done = f32[32,128,256]{2,1,0:T(8,128)} async-done(((f32[8,128,256]{2,1,0:T(8,128)}), f32[32,128,256]{2,1,0:T(8,128)}) %all-gather.15.cloned.1.call-update) | async-done | bytes 4194320 | tf_op jit(solution)/shard_map/all_gather | solution.py:14
  114.9 149.8 %all-gather.13.cloned.1.call-done = f32[32,256,256]{2,1,0:T(8,128)} async-done(((f32[8,256,256]{2,1,0:T(8,128)}), f32[32,256,256]{2,1,0:T(8,128)}) %all-gather.13.cloned.1.call-update) | async-done | bytes 8388624 | tf_op jit(solution)/shard_map/all_gather | solution.py:14
  264.8 49.5 %while.30 = (s32[]{:T(128)}, f32[8,256,256]{1,2,0:T(8,128)S(1)}, f32[8,128,256]{1,2,0:T(8,128)}, s32[]{:T(128)}, f32[4,8,256,256]{3,2,1,0:T(8,128)}, /*index=5*/f32[4,8,128,256]{3,2,1,0:T(8,128)}, s32[]{:T(128)}, s32[]{:T(128)}) while((s32[]{:T(128)}, f32[8,256,256]{1,2,0:T(8,128)S(1)}, f32[8,128,256]{1,2,0:T(8,128)}, s32[]{:T(128)}, ...), condition=%wide.region_7.8_spmd.clone, body=%wide.region_6.7_spmd.clone.sunk | while | flops 2417491968 | bytes 25168492 | solution.py:23
  264.8 2.3 constant_dynamic-slice_fusion.5
  269.9 6.1 fusion.111
  276.2 5.1 bitcast_select_fusion.2
  281.3 2.3 constant_dynamic-slice_fusion.5
  286.4 6.1 fusion.111
  292.7 5.1 bitcast_select_fusion.2
  297.8 2.3 constant_dynamic-slice_fusion.5
  302.9 6.1 fusion.111
  309.1 5.1 bitcast_select_fusion.2
  314.3 5.0 fusion.48
  319.3 2.6 copy.129
  322.2 6.0 convolution_select_fusion
  328.3 72.8 %all-gather.21.cloned.1.call-done = f32[32,128,256]{2,1,0:T(8,128)} async-done(((f32[8,128,256]{2,1,0:T(8,128)}), f32[32,128,256]{2,1,0:T(8,128)}) %all-gather.21.cloned.1.call-update) | async-done | bytes 4194320 | tf_op jit(solution)/shard_map/all_gather | solution.py:8
  401.1 3.6 reduce_sum.39
  404.8 145.9 %all-gather.17.cloned.1.call-done = f32[32,256,256]{2,1,0:T(8,128)} async-done(((f32[8,256,256]{2,1,0:T(8,128)}), f32[32,256,256]{2,1,0:T(8,128)}) %all-gather.17.cloned.1.call-update) | async-done | bytes 8388624 | tf_op jit(solution)/shard_map/all_gather | solution.py:8
  550.8 5.6 reduce_sum.38
  561.1 4.9 fusion.65
  567.3 17.6 %all-gather.23.cloned.1.call-done = f32[32,128,256]{2,1,0:T(8,128)} async-done(((f32[8,128,256]{2,1,0:T(8,128)}), f32[32,128,256]{2,1,0:T(8,128)}) %all-gather.23.cloned.1.call-update) | async-done | bytes 4194320 | tf_op jit(solution)/shard_map/all_gather | solution.py:143
  584.9 59.7 %all-gather.19.cloned.1.call-done = f32[32,256,256]{2,1,0:T(8,128)} async-done(((f32[8,256,256]{2,1,0:T(8,128)}), f32[32,256,256]{2,1,0:T(8,128)}) %all-gather.19.cloned.1.call-update) | async-done | bytes 8388624 | tf_op jit(solution)/shard_map/all_gather | solution.py:142
  644.6 41.4 %while.29 = (s32[]{:T(128)}, f32[8,128,256]{1,2,0:T(8,128)}, s32[]{:T(128)}, f32[4,8,256,256]{3,2,1,0:T(8,128)}, f32[4,8,128,256]{3,2,1,0:T(8,128)}, /*index=5*/s32[]{:T(128)}) while((s32[]{:T(128)}, f32[8,128,256]{1,2,0:T(8,128)}, s32[]{:T(128)}, f32[4,8,256,256]{3,2,1,0:T(8,128)}, f32[4,8,128,256]{3,2,1,0:T(8,128)}, ...), condition=%wide.region_11.12_spmd, body=%wide.region_10.11_spmd.sunk | while | flops 805830656 | bytes 16777840 | solution.py:124
  649.1 6.1 fusion.106
  659.4 6.1 fusion.106
  669.7 6.1 fusion.106
  680.0 6.1 fusion.106
  686.1 4.0 convolution_add_fusion
  693.1 2.6 fusion.45
  (158 shorter events, 63.5 us)
Async XLA Ops:
  6.5 108.3 %all-gather.15.cloned.1.call-start = ((), (), s32[]{:S(2)}) async-start(), calls=%async_computation.1 | async-start | bytes 5242880 | tf_op jit(solution)/shard_map/all_gather | solution.py:14
  6.6 6.9 copy-start.23
  8.2 5.3 copy-start.26
  10.5 4.3 copy-start.29
  10.5 4.4 copy-start.25
  10.5 4.6 copy-start.19
  17.7 2.1 copy-start.21
  19.9 16.1 %copy-start.2 = (f32[256,8,128]{2,1,0:T(8,128)}, f32[256,8,128]{2,1,0:T(8,128)S(1)}, u32[]{:S(2)}) copy-start(f32[256,8,128]{2,1,0:T(8,128)S(1)} %get-tuple-element.269) | copy-start | bytes 3145732
  24.2 1.7 copy-start.6
  28.6 3.0 copy-start.30
  28.6 3.0 copy-start.24
  28.6 3.0 copy-start.27
  28.6 3.0 copy-start.28
  31.3 233.4 %all-gather.13.cloned.1.call-start = ((), (), s32[]{:S(2)}) async-start(), calls=%async_computation | async-start | bytes 10485760 | tf_op jit(solution)/shard_map/all_gather | solution.py:14
  34.5 2.9 copy-start.8
  34.5 2.9 copy-start.10
  35.9 1.5 copy-start.12
  40.2 361.0 %all-gather.21.cloned.1.call-start = ((), (), s32[]{:S(2)}) async-start(), calls=%async_computation.4 | async-start | bytes 5242880 | tf_op jit(solution)/shard_map/all_gather | solution.py:8
  319.3 2.9 copy-start.9
  319.3 2.9 copy-start.11
  322.0 228.8 %all-gather.17.cloned.1.call-start = ((), (), s32[]{:S(2)}) async-start(), calls=%async_computation.2 | async-start | bytes 10485760 | tf_op jit(solution)/shard_map/all_gather | solution.py:8
  328.2 256.7 %all-gather.23.cloned.1.call-start = ((), (), s32[]{:S(2)}) async-start(), calls=%async_computation.5 | async-start | bytes 5242880 | tf_op jit(solution)/shard_map/all_gather | solution.py:143
  404.8 239.9 %all-gather.19.cloned.1.call-start = ((), (), s32[]{:S(2)}) async-start(), calls=%async_computation.3 | async-start | bytes 10485760 | tf_op jit(solution)/shard_map/all_gather | solution.py:142
  556.3 2.1 copy-start.22
  561.1 4.9 copy-start.1
  647.5 1.5 copy-start
  657.8 1.5 copy-start
  668.1 1.5 copy-start
  678.4 1.5 copy-start
  686.1 4.0 copy-start.4
  690.1 2.5 copy-start.15
  691.4 1.7 copy-start.5
  (8 other events, 8.5 us)
Sparse Core Ops, SparseCore 0:
  31.4 83.4 all-gather.14
  116.4 148.1 all-gather.12
  322.1 78.9 all-gather.20
  402.6 148.1 all-gather.16
  552.2 32.6 all-gather.22
  586.3 58.2 all-gather.18
